TPU v7x, 256 devices: a whole 4x4x8 slice. The times are simulated.
256 devices in a mesh: ent: 64 (over z, y, core), rel: 4 (over x).
Axes of the slice: x: 4, y: 4, z: 8, core: 2. Of those that a mesh axis runs over, the one named last changes fastest.
Arguments:
- entity_rows: bfloat16 [65536, 256], P('ent'), may hold values from -2.5 to 2.5
- request_rows: int32 [64, 64, 32], P('ent'), may hold values from 0 to 1023
- edge_heads: int32 [262144], P(('ent', 'rel')), may hold values from 0 to 1023
- edge_rels: int32 [262144], P(('ent', 'rel')), may hold values from 0 to 7
- edge_tails: int32 [262144], P(('ent', 'rel')), may hold values from 0 to 2047
- edge_counts: int32 [256], P(('ent', 'rel')), may hold values from 1 to 1024, 163840 in all
- negative_rows: int32 [65536], P(('ent', 'rel')), may hold values from 0 to 1023
- relation_blocks: bfloat16 [32, 8, 32, 32], P('rel'), may hold values from -1 to 1
Outputs:
- entity_grad: float32 [65536, 256], P('ent')
- relation_grad: float32 [32, 8, 32, 32], P('rel')
Inputs may be any that keep to these rules, and one draw needn't show every extreme that they name: Edge slots of bucket b at or past edge_counts[b] are ignored; some bucket is full in every draw.
All inputs are finite; a program needn't handle non-finite values. No bound on the sum of `edge_counts` on one device may be relied on, other than what follows from the above.
Results may differ from a plain program's by a relative error of at most 0.009.
Values may be sent and summed in bfloat16 or wider, within the bound.
No kernel may reach another device: no remote copies, remote signals or barrier semaphores. Data moves between devices by JAX's collectives and lax.ppermute only.
A program may use at most 64 MiB of HBM per device.

v0:
```python
import math
import jax
import jax.numpy as jnp
from jax import lax
from jax.sharding import PartitionSpec as P


def pick_rows(indices, source_table):
    row_total = indices.shape[0]
    block_size = math.gcd(row_total, 256)
    grouped = indices.reshape(row_total // block_size, block_size)
    columns = jnp.arange(source_table.shape[0], dtype=jnp.int32)

    def pick_block(index_block):
        one_hot = (index_block[:, None] == columns[None, :]).astype(jnp.bfloat16)
        return jnp.dot(one_hot, source_table, preferred_element_type=jnp.float32).astype(
            jnp.bfloat16
        )

    picked = lax.map(pick_block, grouped)
    return picked.reshape(row_total, source_table.shape[1])


def owner_add(indices, gradients, entity_count):
    start_value = jnp.zeros((entity_count, gradients.shape[1]), jnp.float32)
    return start_value.at[indices].add(gradients)


def local(
    entity_rows,
    request_rows,
    edge_heads,
    edge_rels,
    edge_tails,
    edge_counts,
    negative_rows,
    relation_blocks,
):
    entity_count, feature_width = entity_rows.shape
    part_count = request_rows.shape[1]
    slot_count = request_rows.shape[2]
    r_count, block_count, block_width = (
        relation_blocks.shape[0],
        relation_blocks.shape[1],
        relation_blocks.shape[2],
    )
    neg_count = negative_rows.shape[0]
    owner_lists = lax.all_to_all(request_rows, "ent", split_axis=1, concat_axis=0, tiled=True)
    wanted = pick_rows(owner_lists.reshape(-1), entity_rows).reshape(
        part_count, 1, slot_count, feature_width
    )
    fetched = lax.all_to_all(wanted, "ent", split_axis=0, concat_axis=1, tiled=True)
    fetched = fetched.reshape(part_count * slot_count, feature_width)
    neg_rows = pick_rows(negative_rows, entity_rows)
    edge_dev = edge_heads.shape[0]
    block_size = math.gcd(edge_dev, 256)
    block_total = edge_dev // block_size
    live_count = edge_counts[0]
    positions = jnp.arange(edge_dev, dtype=jnp.int32).reshape(block_total, block_size)
    entity_columns = jnp.arange(entity_count, dtype=jnp.int32)
    slot_columns = jnp.arange(part_count * slot_count, dtype=jnp.int32)
    rel_columns = jnp.arange(r_count, dtype=jnp.int32)
    contract_rows = (((0,), (0,)), ((), ()))

    def edge_block(running, block_inputs):
        slot_acc, entity_acc, neg_acc, relation_acc = running
        head_ids, rel_ids, tail_ids, places = block_inputs
        live_mask = (places < live_count).astype(jnp.float32)
        head_hot = (head_ids[:, None] == entity_columns[None, :]).astype(jnp.bfloat16)
        tail_hot = (tail_ids[:, None] == slot_columns[None, :]).astype(jnp.bfloat16)
        head_rows = jnp.dot(head_hot, entity_rows, preferred_element_type=jnp.float32).astype(
            jnp.bfloat16
        )
        tail_rows = jnp.dot(tail_hot, fetched, preferred_element_type=jnp.float32).astype(
            jnp.bfloat16
        )
        rel_hot = (rel_ids[:, None] == rel_columns[None, :]).astype(jnp.float32)
        head_split = head_rows.reshape(block_size, block_count, block_width)
        proj_all = jnp.einsum(
            "enb,rnbc->renc", head_split, relation_blocks, preferred_element_type=jnp.float32
        )
        projected = (
            jnp.sum(rel_hot.T[:, :, None, None] * proj_all, 0)
            .reshape(block_size, feature_width)
            .astype(jnp.bfloat16)
        )
        projected_wide = projected.astype(jnp.float32)
        positive = jnp.sum(projected_wide * tail_rows.astype(jnp.float32), -1)
        negative = lax.dot_general(
            projected, neg_rows, (((1,), (1,)), ((), ())), preferred_element_type=jnp.float32
        )
        pos_weight = -live_mask * jax.nn.sigmoid(-positive)
        neg_weight = (live_mask[:, None] * jax.nn.sigmoid(negative) / neg_count).astype(
            jnp.bfloat16
        )
        grad_proj = (
            pos_weight[:, None] * tail_rows.astype(jnp.float32)
            + jnp.dot(neg_weight, neg_rows, preferred_element_type=jnp.float32)
        ).astype(jnp.bfloat16)
        weighted = (pos_weight[:, None] * projected_wide).astype(jnp.bfloat16)
        grad_split = grad_proj.reshape(block_size, block_count, block_width)
        back_all = jnp.einsum(
            "enc,rnbc->renb", grad_split, relation_blocks, preferred_element_type=jnp.float32
        )
        head_grad = (
            jnp.sum(rel_hot.T[:, :, None, None] * back_all, 0)
            .reshape(block_size, feature_width)
            .astype(jnp.bfloat16)
        )
        slot_acc = slot_acc + lax.dot_general(
            tail_hot, weighted, contract_rows, preferred_element_type=jnp.float32
        )
        entity_acc = entity_acc + lax.dot_general(
            head_hot, head_grad, contract_rows, preferred_element_type=jnp.float32
        )
        neg_acc = neg_acc + lax.dot_general(
            neg_weight, projected, contract_rows, preferred_element_type=jnp.float32
        )
        masked_heads = rel_hot.T.astype(jnp.bfloat16)[:, :, None, None] * head_split[None]
        relation_acc = relation_acc + jnp.einsum(
            "renb,enc->rnbc", masked_heads, grad_split, preferred_element_type=jnp.float32
        )
        return ((slot_acc, entity_acc, neg_acc, relation_acc), None)

    start_values = (
        jnp.zeros((part_count * slot_count, feature_width), jnp.float32),
        jnp.zeros((entity_count, feature_width), jnp.float32),
        jnp.zeros((neg_count, feature_width), jnp.float32),
        jnp.zeros(relation_blocks.shape, jnp.float32),
    )
    block_inputs = (
        edge_heads.reshape(block_total, block_size),
        edge_rels.reshape(block_total, block_size),
        edge_tails.reshape(block_total, block_size),
        positions,
    )
    (slot_acc, entity_acc, neg_acc, relation_acc), _ = lax.scan(
        edge_block, start_values, block_inputs
    )
    neg_hot = (negative_rows[:, None] == entity_columns[None, :]).astype(jnp.bfloat16)
    entity_acc = entity_acc + lax.dot_general(
        neg_hot, neg_acc.astype(jnp.bfloat16), contract_rows, preferred_element_type=jnp.float32
    )
    slot_grads = slot_acc.reshape(1, part_count, slot_count, feature_width)
    returned = lax.all_to_all(
        slot_grads.astype(jnp.bfloat16), "ent", split_axis=1, concat_axis=0, tiled=True
    ).astype(slot_grads.dtype)
    entity_acc = entity_acc + owner_add(
        owner_lists.reshape(-1), returned.reshape(-1, feature_width), entity_count
    )
    entity_grad = lax.psum(entity_acc, "rel")
    relation_grad = lax.psum(relation_acc, "ent")
    return (entity_grad, relation_grad)


def solution(mesh):
    in_specs = (
        P("ent", None),
        P("ent", None, None),
        P(("ent", "rel")),
        P(("ent", "rel")),
        P(("ent", "rel")),
        P(("ent", "rel")),
        P(("ent", "rel")),
        P("rel", None, None, None),
    )
    out_specs = (P("ent", None), P("rel", None, None, None))
    return jax.shard_map(local, mesh=mesh, in_specs=in_specs, out_specs=out_specs, check_vma=False)
```

profile of v0, /device:TPU:8, one launch (start us, length us, event | category | flops | bytes accessed | tf_op | source)
XLA Modules:
  0.0 383.0 jit_solution(16212449031649504692)
XLA Ops:
  8.6 12.1 %all-to-all-start = ((s32[1,64,32]{2,0,1:T(1,128)}), s32[1,64,32]{2,0,1:T(1,128)S(1)}, u32[]{:S(2)}, u32[]{:S(2)}) async-start(s32[1,64,32]{2,0,1:T(1,128)} %copy.20), calls=%async_computation | async-start | bytes 65536 | tf_op jit(solution)/shard_map/all_to_all | solution.py:48
  20.7 8.5 %all-to-all-done = s32[1,64,32]{2,0,1:T(1,128)S(1)} async-done(((s32[1,64,32]{2,0,1:T(1,128)}), s32[1,64,32]{2,0,1:T(1,128)S(1)}, u32[]{:S(2)}, u32[]{:S(2)}) %all-to-all-start) | async-done | bytes 8224 | tf_op jit(solution)/shard_map/all_to_all | solution.py:48
  30.6 16.5 %while.32 = (s32[]{:T(128)}, bf16[8,256,256]{2,1,0:T(8,128)(2,1)}, s32[8,256]{1,0:T(8,128)S(1)}, bf16[1024,256]{1,0:T(8,128)(2,1)}, s32[]{:T(128)}) while((s32[]{:T(128)}, bf16[8,256,256]{2,1,0:T(8,128)(2,1)}, s32[8,256]{1,0:T(8,128)S(1)}, bf16[1024,256]{1,0:T(8,128)(2,1)}, s32[]{:T(128)}) %tuple.56), condition=%wide.region_1.2_spmd.clone, body=%wide.region_0.1_spmd.clone.sunk | while | flops 134545408 | bytes 658509 | solution.py:20
  30.6 2.1 fusion.90
  32.6 2.0 fusion.90
  34.7 2.0 fusion.90
  36.8 2.1 fusion.90
  38.8 2.1 fusion.90
  40.9 2.0 fusion.90
  42.9 2.0 fusion.90
  45.0 2.1 fusion.90
  47.0 6.5 %all-to-all-start.1 = ((bf16[64,1,32,256]{3,2,1,0:T(8,128)(2,1)}), bf16[64,1,32,256]{3,2,1,0:T(8,128)(2,1)}, u32[]{:S(2)}, u32[]{:S(2)}) async-start(bf16[64,1,32,256]{3,2,1,0:T(8,128)(2,1)} %bitcast.1), calls=%async_computation.1 | async-start | bytes 2097152 | tf_op jit(solution)/shard_map/all_to_all | solution.py:52
  56.9 25.4 %all-to-all-done.1 = bf16[64,1,32,256]{3,2,1,0:T(8,128)(2,1)} async-done(((bf16[64,1,32,256]{3,2,1,0:T(8,128)(2,1)}), bf16[64,1,32,256]{3,2,1,0:T(8,128)(2,1)}, u32[]{:S(2)}, u32[]{:S(2)}) %all-to-all-start.1) | async-done | bytes 1048608 | tf_op jit(solution)/shard_map/all_to_all | solution.py:52
  82.3 38.9 %while.33 = (s32[]{:T(128)}, f32[2048,256]{1,0:T(8,128)S(1)}, f32[1024,256]{1,0:T(8,128)S(1)}, f32[256,256]{1,0:T(8,128)S(1)}, f32[8,8,32,32]{2,3,0,1:T(8,128)},...) while((s32[]{:T(128)}, f32[2048,256]{1,0:T(8,128)S(1)}, ...), condition=%wide.region_6.7_spmd.clone, body=%wide.region_2.6_spmd.clone.sunk | while | flops 1016077568 | bytes 14733582 | solution.py:137
  86.6 2.1 fusion.111
  96.4 2.1 fusion.111
  106.1 2.1 fusion.111
  115.8 2.1 fusion.111
  122.3 5.9 %all-to-all-start.2 = ((bf16[1,64,32,256]{3,2,0,1:T(8,128)(2,1)}), bf16[1,64,32,256]{3,2,0,1:T(8,128)(2,1)S(1)}, u32[]{:S(2)}, u32[]{:S(2)}) async-start(bf16[1,64,32,256]{3,2,0,1:T(8,128)(2,1)} %bitcast.124), calls=%async_computation.2 | async-start | bytes 2097152 | tf_op jit(solution)/shard_map/all_to_all | solution.py:145
  130.4 27.4 %all-to-all-done.2 = bf16[1,64,32,256]{3,2,0,1:T(8,128)(2,1)S(1)} async-done(((bf16[1,64,32,256]{3,2,0,1:T(8,128)(2,1)}), bf16[1,64,32,256]{3,2,0,1:T(8,128)(2,1)S(1)}, u32[]{:S(2)}, u32[]{:S(2)}) %all-to-all-start.2) | async-done | bytes 1048608 | tf_op jit(solution)/shard_map/all_to_all | solution.py:145
  157.7 12.0 %scatter_custom_fusion = f32[1024,256]{1,0:T(8,128)S(1)} fusion(f32[1024,256]{1,0:T(8,128)S(1)} %convolution_add_fusion.4, s32[2048]{0:T(1024)S(1)} %bitcast.138, bf16[2048,256]{1,0:T(8,128)(2,1)S(1)} %bitcast.125), kind=kCustom, calls=%fused_computation.57 | custom fusion | flops 1048576 | bytes 2097152 | tf_op jit(solution)/shard_map/scatter-add | solution.py:26
  170.8 150.9 %all-reduce.5.cloned.1.call-done = f32[8,8,32,32]{3,2,1,0:T(8,128)} async-done(((f32[8,8,32,32]{3,2,1,0:T(8,128)}), f32[8,8,32,32]{3,2,1,0:T(8,128)}) %all-reduce.5.cloned.1.call-update) | async-done | bytes 262160 | tf_op jit(solution)/shard_map/psum | solution.py:152
  321.6 51.3 %all-reduce.3.cloned.1.call-done = f32[1024,256]{1,0:T(8,128)} async-done(((f32[1024,256]{1,0:T(8,128)}), f32[1024,256]{1,0:T(8,128)}) %all-reduce.3.cloned.1.call-update) | async-done | bytes 1048592 | tf_op jit(solution)/shard_map/psum | solution.py:151
  372.9 2.3 copy.51
  (131 shorter events, 41.3 us)
Async XLA Ops:
  8.6 20.7 %all-to-all-start = ((s32[1,64,32]{2,0,1:T(1,128)}), s32[1,64,32]{2,0,1:T(1,128)S(1)}, u32[]{:S(2)}, u32[]{:S(2)}) async-start(s32[1,64,32]{2,0,1:T(1,128)} %copy.20), calls=%async_computation | async-start | bytes 65536 | tf_op jit(solution)/shard_map/all_to_all | solution.py:48
  47.0 6.5 %copy-start.8 = (s32[1024]{0:T(1024)S(1)}, s32[1024]{0:T(1024)}, u32[]{:S(2)}) copy-start(s32[1024]{0:T(1024)} %param.14) | copy-start | bytes 12292
  47.0 6.5 %copy-start.9 = (s32[1024]{0:T(1024)S(1)}, s32[1024]{0:T(1024)}, u32[]{:S(2)}) copy-start(s32[1024]{0:T(1024)} %param.15) | copy-start | bytes 12292
  47.0 6.6 %copy-start.10 = (s32[1024]{0:T(1024)S(1)}, s32[1024]{0:T(1024)}, u32[]{:S(2)}) copy-start(s32[1024]{0:T(1024)} %param.16) | copy-start | bytes 12292
  47.0 35.3 %all-to-all-start.1 = ((bf16[64,1,32,256]{3,2,1,0:T(8,128)(2,1)}), bf16[64,1,32,256]{3,2,1,0:T(8,128)(2,1)}, u32[]{:S(2)}, u32[]{:S(2)}) async-start(bf16[64,1,32,256]{3,2,1,0:T(8,128)(2,1)} %bitcast.1), calls=%async_computation.1 | async-start | bytes 2097152 | tf_op jit(solution)/shard_map/all_to_all | solution.py:52
  86.4 2.6 copy-start.5
  86.6 2.8 copy-start
  90.4 1.7 copy-start.1
  96.1 2.6 copy-start.5
  96.4 2.8 copy-start
  100.1 1.7 copy-start.1
  105.8 2.6 copy-start.5
  106.1 2.8 copy-start
  109.8 1.7 copy-start.1
  115.6 2.6 copy-start.5
  115.8 2.8 copy-start
  119.6 1.7 copy-start.1
  121.2 7.0 %copy-start.7 = (s32[1,64,32]{2,0,1:T(1,128)S(1)}, s32[1,64,32]{2,0,1:T(1,128)}, u32[]{:S(2)}) copy-start(s32[1,64,32]{2,0,1:T(1,128)} %copy-done.6) | copy-start | bytes 24580
  122.3 6.0 %copy-start.2 = (f32[8,8,32,32]{2,3,0,1:T(8,128)S(1)}, f32[8,8,32,32]{2,3,0,1:T(8,128)}, u32[]{:S(2)}) copy-start(f32[8,8,32,32]{2,3,0,1:T(8,128)} %get-tuple-element.138) | copy-start | bytes 786436
  122.3 35.4 %all-to-all-start.2 = ((bf16[1,64,32,256]{3,2,0,1:T(8,128)(2,1)}), bf16[1,64,32,256]{3,2,0,1:T(8,128)(2,1)S(1)}, u32[]{:S(2)}, u32[]{:S(2)}) async-start(bf16[1,64,32,256]{3,2,0,1:T(8,128)(2,1)} %bitcast.124), calls=%async_computation.2 | async-start | bytes 2097152 | tf_op jit(solution)/shard_map/all_to_all | solution.py:145
  128.2 1.6 copy-start.11
  128.2 193.4 %all-reduce.5.cloned.1.call-start = ((), (), s32[]{:S(2)}) async-start(), calls=%async_computation.4 | async-start | bytes 2097152 | tf_op jit(solution)/shard_map/psum | solution.py:152
  129.8 243.2 %all-reduce.3.cloned.1.call-start = ((), (), s32[]{:S(2)}) async-start(), calls=%async_computation.3 | async-start | bytes 2097152 | tf_op jit(solution)/shard_map/psum | solution.py:151
  321.6 53.6 %copy-start.4 = (f32[8,8,32,32]{3,2,1,0:T(8,128)S(1)}, f32[8,8,32,32]{3,2,1,0:T(8,128)}, u32[]{:S(2)}) copy-start(f32[8,8,32,32]{3,2,1,0:T(8,128)} %all-reduce.5.cloned.1.call-done) | copy-start | bytes 786436
  (2 other events, 2.3 us)
Sparse Core Ops, SparseCore 0:
  132.4 189.1 all-reduce.4
  324.6 48.3 all-reduce.2
where the time goes:
time: 384 us; the launch traced here: 383 us
  waiting for transfers between devices  263 us (68%)
  matrix products  53.8 us (14%)
  starting transfers between devices  24.5 us (6%)
  other arithmetic  16.5 us (4%)
  between operations  14.2 us (4%)
  local copies, waits for them, and re-layouts  9.81 us (3%)
    psum x1, waiting for transfers between devices, local(): relation_grad = lax.psum(relation_acc, 'ent')  151 us
    psum x1, waiting for transfers between devices, local(): entity_grad = lax.psum(entity_acc, 'rel')  51.3 us
    all_to_all x1, waiting for transfers between devices, local(): lax.all_to_all(slot_grads.astype(jnp.bfloat16), 'ent', split_axis=1, conc...  27.4 us
    all_to_all x1, waiting for transfers between devices, local(): lax.all_to_all(wanted, 'ent', split_axis=0, concat_axis=1, tiled=True)  25.4 us
    dot_general x9, matrix products, pick_block(): jnp.dot(one_hot, source_table, preferred_element_type=jnp.float32)  17.8 us
    all_to_all x1, starting transfers between devices, local(): lax.all_to_all(request_rows, 'ent', split_axis=1, concat_axis=0, tiled=True)  12.1 us
    scatter-add x1, other arithmetic, owner_add(): return start_value.at[indices].add(gradients)  12 us
    all_to_all x1, waiting for transfers between devices, local(): lax.all_to_all(request_rows, 'ent', split_axis=1, concat_axis=0, tiled=True)  8.54 us
  transfers between devices with their start and end apart: 5, of which 5 were waited for; matrix products, arithmetic and copies ran while one was open for 5% of the time, Pallas kernels for 0%

commit v1 on v0

--- a/solution.py
+++ b/solution.py
@@ -142,8 +142,14 @@
         neg_hot, neg_acc.astype(jnp.bfloat16), contract_rows, preferred_element_type=jnp.float32
     )
     slot_grads = slot_acc.reshape(1, part_count, slot_count, feature_width)
-    returned = lax.all_to_all(
-        slot_grads.astype(jnp.bfloat16), "ent", split_axis=1, concat_axis=0, tiled=True
+    returned = jnp.concatenate(
+        lax.all_to_all(
+            jnp.stack(jnp.split(slot_grads.astype(jnp.bfloat16), lax.axis_size("ent"), axis=1)),
+            "ent",
+            0,
+            0,
+        ),
+        axis=0,
     ).astype(slot_grads.dtype)
     entity_acc = entity_acc + owner_add(
         owner_lists.reshape(-1), returned.reshape(-1, feature_width), entity_count

time: 384 us -> 422 us (1.099)
  local copies, waits for them, and re-layouts: 9.81 us -> 48.6 us
    unnamed x22 -> x85, local copies, waits for them, and re-layouts: 7.54 us -> 45.7 us
  transfers between devices with their start and end apart: 5 -> 5, of which waited for: 5 -> 5; matrix products, arithmetic and copies ran while one was open for 5% -> 4% of each run, Pallas kernels for 0% -> 0%
where the time goes in v1:
time: 422 us; the launch traced here: 421 us
  waiting for transfers between devices  263 us (62%)
  matrix products  53.8 us (13%)
  local copies, waits for them, and re-layouts  48.6 us (12%)
  starting transfers between devices  24.4 us (6%)
  other arithmetic  15.7 us (4%)
  between operations  14.3 us (3%)
    psum x1, waiting for transfers between devices, local(): relation_grad = lax.psum(relation_acc, 'ent')  151 us
    psum x1, waiting for transfers between devices, local(): entity_grad = lax.psum(entity_acc, 'rel')  51.3 us
    unnamed x85, local copies, waits for them, and re-layouts  45.7 us
    all_to_all x1, waiting for transfers between devices, local(): lax.all_to_all(jnp.stack(jnp.split(slot_grads.astype(jnp.bfloat16), lax.a...  27.4 us
    all_to_all x1, waiting for transfers between devices, local(): lax.all_to_all(wanted, 'ent', split_axis=0, concat_axis=1, tiled=True)  25.4 us
    dot_general x9, matrix products, pick_block(): jnp.dot(one_hot, source_table, preferred_element_type=jnp.float32)  17.8 us
    scatter-add x1, other arithmetic, owner_add(): return start_value.at[indices].add(gradients)  12.2 us
    all_to_all x1, starting transfers between devices, local(): lax.all_to_all(request_rows, 'ent', split_axis=1, concat_axis=0, tiled=True)  12.1 us
  transfers between devices with their start and end apart: 5, of which 5 were waited for; matrix products, arithmetic and copies ran while one was open for 4% of the time, Pallas kernels for 0%

profile of v1, /device:TPU:8, one launch (start us, length us, event | category | flops | bytes accessed | tf_op | source)
XLA Modules:
  0.0 420.8 jit_solution(12543262863781457874)
XLA Ops:
  8.6 12.1 %all-to-all-start = ((s32[1,64,32]{2,0,1:T(1,128)}), s32[1,64,32]{2,0,1:T(1,128)S(1)}, u32[]{:S(2)}, u32[]{:S(2)}) async-start(s32[1,64,32]{2,0,1:T(1,128)} %copy.146), calls=%async_computation | async-start | bytes 65536 | tf_op jit(solution)/shard_map/all_to_all | solution.py:48
  20.7 8.5 %all-to-all-done = s32[1,64,32]{2,0,1:T(1,128)S(1)} async-done(((s32[1,64,32]{2,0,1:T(1,128)}), s32[1,64,32]{2,0,1:T(1,128)S(1)}, u32[]{:S(2)}, u32[]{:S(2)}) %all-to-all-start) | async-done | bytes 8224 | tf_op jit(solution)/shard_map/all_to_all | solution.py:48
  30.6 16.5 %while.32 = (s32[]{:T(128)}, bf16[8,256,256]{2,1,0:T(8,128)(2,1)}, s32[8,256]{1,0:T(8,128)S(1)}, bf16[1024,256]{1,0:T(8,128)(2,1)}, s32[]{:T(128)}) while((s32[]{:T(128)}, bf16[8,256,256]{2,1,0:T(8,128)(2,1)}, s32[8,256]{1,0:T(8,128)S(1)}, bf16[1024,256]{1,0:T(8,128)(2,1)}, s32[]{:T(128)}) %tuple.56), condition=%wide.region_1.2_spmd.clone, body=%wide.region_0.1_spmd.clone.sunk | while | flops 134545408 | bytes 658509 | solution.py:20
  30.6 2.1 fusion.90
  32.6 2.1 fusion.90
  34.7 2.1 fusion.90
  36.8 2.0 fusion.90
  38.8 2.0 fusion.90
  40.9 2.1 fusion.90
  42.9 2.1 fusion.90
  45.0 2.0 fusion.90
  47.0 6.5 %all-to-all-start.1 = ((bf16[64,1,32,256]{3,2,1,0:T(8,128)(2,1)}), bf16[64,1,32,256]{3,2,1,0:T(8,128)(2,1)}, u32[]{:S(2)}, u32[]{:S(2)}) async-start(bf16[64,1,32,256]{3,2,1,0:T(8,128)(2,1)} %bitcast.1), calls=%async_computation.1 | async-start | bytes 2097152 | tf_op jit(solution)/shard_map/all_to_all | solution.py:52
  56.9 25.4 %all-to-all-done.1 = bf16[64,1,32,256]{3,2,1,0:T(8,128)(2,1)} async-done(((bf16[64,1,32,256]{3,2,1,0:T(8,128)(2,1)}), bf16[64,1,32,256]{3,2,1,0:T(8,128)(2,1)}, u32[]{:S(2)}, u32[]{:S(2)}) %all-to-all-start.1) | async-done | bytes 1048608 | tf_op jit(solution)/shard_map/all_to_all | solution.py:52
  82.3 38.9 %while.33 = (s32[]{:T(128)}, f32[2048,256]{1,0:T(8,128)S(1)}, f32[1024,256]{1,0:T(8,128)S(1)}, f32[256,256]{1,0:T(8,128)S(1)}, f32[8,8,32,32]{2,3,0,1:T(8,128)},...) while((s32[]{:T(128)}, f32[2048,256]{1,0:T(8,128)S(1)}, ...), condition=%wide.region_6.7_spmd.clone, body=%wide.region_2.6_spmd.clone.sunk | while | flops 1016077568 | bytes 14733582 | solution.py:137
  86.6 2.1 fusion.111
  96.4 2.1 fusion.111
  106.1 2.1 fusion.111
  115.8 2.1 fusion.111
  160.2 5.7 %all-to-all-start.2 = ((bf16[64,1,1,32,256]{4,3,2,1,0:T(8,128)(2,1)}), bf16[64,1,1,32,256]{4,3,2,1,0:T(8,128)(2,1)S(1)}, u32[]{:S(2)}, u32[]{:S(2)}) async-start(bf16[64,1,1,32,256]{4,3,2,1,0:T(8,128)(2,1)} %constant_dynamic-update-slice_fusion), calls=%async_computation.2 | async-start | bytes 2097152 | tf_op jit(solution)/shard_map/all_to_all | solution.py:146
  168.1 27.4 %all-to-all-done.2 = bf16[64,1,1,32,256]{4,3,2,1,0:T(8,128)(2,1)S(1)} async-done(((bf16[64,1,1,32,256]{4,3,2,1,0:T(8,128)(2,1)}), bf16[64,1,1,32,256]{4,3,2,1,0:T(8,128)(2,1)S(1)}, u32[]{:S(2)}, u32[]{:S(2)}) %all-to-all-start.2) | async-done | bytes 1048608 | tf_op jit(solution)/shard_map/all_to_all | solution.py:146
  195.5 12.2 %scatter_custom_fusion = f32[1024,256]{1,0:T(8,128)S(1)} fusion(f32[1024,256]{1,0:T(8,128)S(1)} %convolution_add_fusion.4, s32[2048]{0:T(1024)S(1)} %bitcast.457, bf16[2048,256]{1,0:T(8,128)(2,1)S(1)} %bitcast.380), kind=kCustom, calls=%fused_computation.57 | custom fusion | flops 1048576 | bytes 2097152 | tf_op jit(solution)/shard_map/scatter-add | solution.py:26
  208.7 150.7 %all-reduce.5.cloned.1.call-done = f32[8,8,32,32]{3,2,1,0:T(8,128)} async-done(((f32[8,8,32,32]{3,2,1,0:T(8,128)}), f32[8,8,32,32]{3,2,1,0:T(8,128)}) %all-reduce.5.cloned.1.call-update) | async-done | bytes 262160 | tf_op jit(solution)/shard_map/psum | solution.py:158
  359.4 51.3 %all-reduce.3.cloned.1.call-done = f32[1024,256]{1,0:T(8,128)} async-done(((f32[1024,256]{1,0:T(8,128)}), f32[1024,256]{1,0:T(8,128)}) %all-reduce.3.cloned.1.call-update) | async-done | bytes 1048592 | tf_op jit(solution)/shard_map/psum | solution.py:157
  410.7 2.3 copy.240
  (195 shorter events, 79.1 us)
Async XLA Ops:
  8.6 20.7 %all-to-all-start = ((s32[1,64,32]{2,0,1:T(1,128)}), s32[1,64,32]{2,0,1:T(1,128)S(1)}, u32[]{:S(2)}, u32[]{:S(2)}) async-start(s32[1,64,32]{2,0,1:T(1,128)} %copy.146), calls=%async_computation | async-start | bytes 65536 | tf_op jit(solution)/shard_map/all_to_all | solution.py:48
  47.0 6.5 %copy-start.8 = (s32[1024]{0:T(1024)S(1)}, s32[1024]{0:T(1024)}, u32[]{:S(2)}) copy-start(s32[1024]{0:T(1024)} %param.14) | copy-start | bytes 12292
  47.0 6.5 %copy-start.9 = (s32[1024]{0:T(1024)S(1)}, s32[1024]{0:T(1024)}, u32[]{:S(2)}) copy-start(s32[1024]{0:T(1024)} %param.15) | copy-start | bytes 12292
  47.0 6.6 %copy-start.10 = (s32[1024]{0:T(1024)S(1)}, s32[1024]{0:T(1024)}, u32[]{:S(2)}) copy-start(s32[1024]{0:T(1024)} %param.16) | copy-start | bytes 12292
  47.0 35.3 %all-to-all-start.1 = ((bf16[64,1,32,256]{3,2,1,0:T(8,128)(2,1)}), bf16[64,1,32,256]{3,2,1,0:T(8,128)(2,1)}, u32[]{:S(2)}, u32[]{:S(2)}) async-start(bf16[64,1,32,256]{3,2,1,0:T(8,128)(2,1)} %bitcast.1), calls=%async_computation.1 | async-start | bytes 2097152 | tf_op jit(solution)/shard_map/all_to_all | solution.py:52
  86.3 2.6 copy-start.5
  86.6 2.8 copy-start
  90.3 1.7 copy-start.1
  96.1 2.6 copy-start.5
  96.4 2.8 copy-start
  100.1 1.7 copy-start.1
  105.8 2.6 copy-start.5
  106.1 2.8 copy-start
  109.8 1.7 copy-start.1
  115.6 2.6 copy-start.5
  115.8 2.8 copy-start
  119.6 1.7 copy-start.1
  121.3 44.6 %copy-start.7 = (s32[1,64,32]{2,0,1:T(1,128)S(1)}, s32[1,64,32]{2,0,1:T(1,128)}, u32[]{:S(2)}) copy-start(s32[1,64,32]{2,0,1:T(1,128)} %copy-done.6) | copy-start | bytes 24580
  122.6 43.5 %copy-start.2 = (f32[8,8,32,32]{2,3,0,1:T(8,128)S(1)}, f32[8,8,32,32]{2,3,0,1:T(8,128)}, u32[]{:S(2)}) copy-start(f32[8,8,32,32]{2,3,0,1:T(8,128)} %get-tuple-element.138) | copy-start | bytes 786436
  160.2 35.3 %all-to-all-start.2 = ((bf16[64,1,1,32,256]{4,3,2,1,0:T(8,128)(2,1)}), bf16[64,1,1,32,256]{4,3,2,1,0:T(8,128)(2,1)S(1)}, u32[]{:S(2)}, u32[]{:S(2)}) async-start(bf16[64,1,1,32,256]{4,3,2,1,0:T(8,128)(2,1)} %constant_dynamic-update-slice_fusion), calls=%async_computation.2 | async-start | bytes 2097152 | tf_op jit(solution)/shard_map/all_to_all | solution.py:146
  165.9 1.6 copy-start.11
  165.9 193.4 %all-reduce.5.cloned.1.call-start = ((), (), s32[]{:S(2)}) async-start(), calls=%async_computation.4 | async-start | bytes 2097152 | tf_op jit(solution)/shard_map/psum | solution.py:158
  167.5 243.2 %all-reduce.3.cloned.1.call-start = ((), (), s32[]{:S(2)}) async-start(), calls=%async_computation.3 | async-start | bytes 2097152 | tf_op jit(solution)/shard_map/psum | solution.py:157
  359.4 53.6 %copy-start.4 = (f32[8,8,32,32]{3,2,1,0:T(8,128)S(1)}, f32[8,8,32,32]{3,2,1,0:T(8,128)}, u32[]{:S(2)}) copy-start(f32[8,8,32,32]{3,2,1,0:T(8,128)} %all-reduce.5.cloned.1.call-done) | copy-start | bytes 786436
  (2 other events, 2.3 us)
Sparse Core Ops, SparseCore 0:
  170.2 189.1 all-reduce.4
  362.3 48.3 all-reduce.2
